TPU v7x, 32 devices: a whole 2x2x4 slice. The times are simulated.
32 devices in a mesh: seq: 16 (over z, x, core), dp: 2 (over y).
Axes of the slice: x: 2, y: 2, z: 4, core: 2. Of those that a mesh axis runs over, the one named last changes fastest.
Arguments:
- queries: bfloat16 [2, 1024, 2048], P(None, 'seq', 'dp'), may hold values from -10 to 10
- key_rows: bfloat16 [2, 1024, 2048], P(None, 'seq', 'dp'), may hold values from -10 to 10
- value_rows: bfloat16 [2, 1024, 2048], P(None, 'seq', 'dp'), may hold values from -6 to 6
- query_tangent: bfloat16 [2, 1024, 2048], P(None, 'seq', 'dp'), may hold values from -6 to 6
- key_tangent: bfloat16 [2, 1024, 2048], P(None, 'seq', 'dp'), may hold values from -6 to 6
- out_adjoint: bfloat16 [2, 1024, 2048], P(None, 'seq', 'dp'), may hold values from -6 to 6
Outputs:
- query_product: bfloat16 [2, 1024, 2048], P(None, 'seq', 'dp')
- key_product: bfloat16 [2, 1024, 2048], P(None, 'seq', 'dp')
- value_product: bfloat16 [2, 1024, 2048], P(None, 'seq', 'dp')
- curvature: float32 [2, 16], replicated
All inputs are finite; a program needn't handle non-finite values.
Results may differ from a plain program's by a relative error of at most 0.0051.
Values may be sent and summed in bfloat16 or wider, within the bound.
A program may use at most 64 MiB of HBM per device.

v0:
```python
import jax
import jax.numpy as jnp
from jax import lax
from jax.sharding import PartitionSpec as P

HEAD_DIM = 128


def inner_rows(left, right):
    return lax.dot_general(
        left, right, (((1,), (1,)), ((), ())), preferred_element_type=jnp.float32
    )


def inner_cols(left, right):
    return lax.dot_general(
        left, right, (((0,), (0,)), ((), ())), preferred_element_type=jnp.float32
    )


def score_block(query, keyset, tquery, tkey, start, block_size):
    factor = HEAD_DIM ** (-0.5)
    stop = start + block_size
    query_block = query[start:stop]
    key_block = keyset[:stop]
    scores = factor * inner_rows(query_block, key_block)
    row_index = start + jnp.arange(block_size)[:, None]
    col_index = jnp.arange(stop)[None, :]
    scores = jnp.where(row_index >= col_index, scores, -jnp.inf)
    top_score = jnp.max(scores, axis=1, keepdims=True)
    weights = jnp.exp(scores - top_score)
    probs = weights / jnp.sum(weights, axis=1, keepdims=True)
    tangent_scores = factor * (
        inner_rows(tquery[start:stop], key_block) + inner_rows(query_block, tkey[:stop])
    )
    mean_tangent = jnp.sum(probs * tangent_scores, axis=1, keepdims=True)
    tangent_probs = probs * (tangent_scores - mean_tangent)
    return (probs, tangent_probs)


def head_work(tensors):
    query, keyset, values_in, tquery, tkey, adjoint = tensors
    factor = HEAD_DIM ** (-0.5)
    length = query.shape[0]
    block_size = min(512, length)
    key_hvp = jnp.zeros((length, HEAD_DIM), jnp.float32)
    value_hvp = jnp.zeros((length, HEAD_DIM), jnp.float32)
    query_parts = []
    for number in range(length // block_size):
        start = number * block_size
        stop = start + block_size
        probs, tangent_probs = score_block(query, keyset, tquery, tkey, start, block_size)
        adj_block = adjoint[start:stop]
        grad_probs = inner_rows(adj_block, values_in[:stop])
        delta = jnp.sum(probs * grad_probs, axis=1, keepdims=True)
        centered = grad_probs - delta
        grad_scores = probs * centered
        tangent_delta = jnp.sum(tangent_probs * grad_probs, axis=1, keepdims=True)
        second_scores = tangent_probs * centered - probs * tangent_delta
        tprob_low = tangent_probs.astype(jnp.bfloat16)
        gscore_low = grad_scores.astype(jnp.bfloat16)
        second_low = second_scores.astype(jnp.bfloat16)
        value_hvp = value_hvp.at[:stop].add(inner_cols(tprob_low, adj_block))
        query_parts.append(
            factor
            * (
                jnp.dot(second_low, keyset[:stop], preferred_element_type=jnp.float32)
                + jnp.dot(gscore_low, tkey[:stop], preferred_element_type=jnp.float32)
            )
        )
        key_hvp = key_hvp.at[:stop].add(
            factor
            * (
                inner_cols(second_low, query[start:stop])
                + inner_cols(gscore_low, tquery[start:stop])
            )
        )
    query_hvp = jnp.concatenate(query_parts, axis=0)
    kappa = jnp.sum(tquery.astype(jnp.float32) * query_hvp) + jnp.sum(
        tkey.astype(jnp.float32) * key_hvp
    )
    return (query_hvp, key_hvp, value_hvp, kappa)


def local(queries, key_rows, value_rows, query_tangent, key_tangent, out_adjoint):
    batch_count = queries.shape[0]
    tokens_here = queries.shape[1]
    local_heads = queries.shape[2] // HEAD_DIM

    def to_items(tensor):
        shaped = tensor.reshape(batch_count, tokens_here, local_heads, HEAD_DIM)
        return jnp.transpose(shaped, (0, 2, 1, 3)).reshape(
            batch_count * local_heads, tokens_here, HEAD_DIM
        )

    parts = (
        lax.all_to_all(to_items(queries), "seq", split_axis=0, concat_axis=1, tiled=True),
        lax.all_to_all(to_items(key_rows), "seq", split_axis=0, concat_axis=1, tiled=True),
        lax.all_to_all(to_items(value_rows), "seq", split_axis=0, concat_axis=1, tiled=True),
        lax.all_to_all(to_items(query_tangent), "seq", split_axis=0, concat_axis=1, tiled=True),
        lax.all_to_all(to_items(key_tangent), "seq", split_axis=0, concat_axis=1, tiled=True),
        lax.all_to_all(to_items(out_adjoint), "seq", split_axis=0, concat_axis=1, tiled=True),
    )
    item_count = parts[0].shape[0]
    item = 0
    tensors = tuple((part[item] for part in parts))
    query_hvp, key_hvp, value_hvp, kappa = head_work(tensors)
    query_items = [query_hvp.astype(jnp.bfloat16)]
    key_items = [key_hvp.astype(jnp.bfloat16)]
    value_items = [value_hvp.astype(jnp.bfloat16)]
    kappas = [kappa]
    returned = (
        lax.all_to_all(jnp.stack(query_items), "seq", split_axis=1, concat_axis=0, tiled=True),
        lax.all_to_all(jnp.stack(key_items), "seq", split_axis=1, concat_axis=0, tiled=True),
        lax.all_to_all(jnp.stack(value_items), "seq", split_axis=1, concat_axis=0, tiled=True),
    )

    def to_tokens(tensor):
        shaped = tensor.reshape(batch_count, local_heads, tokens_here, HEAD_DIM)
        return jnp.transpose(shaped, (0, 2, 1, 3)).reshape(
            batch_count, tokens_here, local_heads * HEAD_DIM
        )

    outputs = tuple((to_tokens(piece) for piece in returned))
    heads_total = local_heads * lax.axis_size("dp")
    batch_index = jnp.arange(batch_count)[:, None]
    head_index = jnp.arange(heads_total)[None, :]
    item = 0
    global_item = lax.axis_index("seq") * item_count + item
    batch_here = global_item // local_heads
    head_here = lax.axis_index("dp") * local_heads + global_item % local_heads
    hit = jnp.logical_and(batch_index == batch_here, head_index == head_here)
    board = jnp.where(hit, kappas[item], 0.0)
    curvature = lax.psum(board, ("seq", "dp"))
    return (outputs[0], outputs[1], outputs[2], curvature)


def solution(mesh):
    return jax.shard_map(
        local,
        mesh=mesh,
        in_specs=(
            P(None, "seq", "dp"),
            P(None, "seq", "dp"),
            P(None, "seq", "dp"),
            P(None, "seq", "dp"),
            P(None, "seq", "dp"),
            P(None, "seq", "dp"),
        ),
        out_specs=(P(None, "seq", "dp"), P(None, "seq", "dp"), P(None, "seq", "dp"), P()),
        check_vma=False,
    )
```

profile of v0, /device:TPU:0, one launch (start us, length us, event | category | flops | bytes accessed | tf_op | source)
XLA Modules:
  0.0 181.6 jit_solution(2033972565623164572)
XLA Ops:
  0.7 1.1 copy.68
  1.8 0.8 copy.50
  2.5 7.4 %all-to-all-start = ((bf16[16,64,128]{2,1,0:T(8,128)(2,1)}), bf16[16,64,128]{2,1,0:T(8,128)(2,1)S(1)}, u32[]{:S(2)}, u32[]{:S(2)}) async-start(bf16[16,64,128]{2,1,0:T(8,128)(2,1)} %bitcast.1), calls=%async_computation | async-start | bytes 524288 | tf_op jit(solution)/shard_map/all_to_all | solution.py:97
  10.0 0.8 copy.51
  10.9 9.0 %all-to-all-done = bf16[16,64,128]{2,1,0:T(8,128)(2,1)S(1)} async-done(((bf16[16,64,128]{2,1,0:T(8,128)(2,1)}), bf16[16,64,128]{2,1,0:T(8,128)(2,1)S(1)}, u32[]{:S(2)}, u32[]{:S(2)}) %all-to-all-start) | async-done | bytes 262176 | tf_op jit(solution)/shard_map/all_to_all | solution.py:97
  19.9 3.5 %all-to-all-start.1 = ((bf16[16,64,128]{2,1,0:T(8,128)(2,1)}), bf16[16,64,128]{2,1,0:T(8,128)(2,1)S(1)}, u32[]{:S(2)}, u32[]{:S(2)}) async-start(bf16[16,64,128]{2,1,0:T(8,128)(2,1)} %bitcast.4), calls=%async_computation.1 | async-start | bytes 524288 | tf_op jit(solution)/shard_map/all_to_all | solution.py:98
  23.5 0.8 copy.52
  24.4 9.0 %all-to-all-done.1 = bf16[16,64,128]{2,1,0:T(8,128)(2,1)S(1)} async-done(((bf16[16,64,128]{2,1,0:T(8,128)(2,1)}), bf16[16,64,128]{2,1,0:T(8,128)(2,1)S(1)}, u32[]{:S(2)}, u32[]{:S(2)}) %all-to-all-start.1) | async-done | bytes 262176 | tf_op jit(solution)/shard_map/all_to_all | solution.py:98
  33.4 3.5 %all-to-all-start.2 = ((bf16[16,64,128]{2,1,0:T(8,128)(2,1)}), bf16[16,64,128]{2,1,0:T(8,128)(2,1)S(1)}, u32[]{:S(2)}, u32[]{:S(2)}) async-start(bf16[16,64,128]{2,1,0:T(8,128)(2,1)} %bitcast.7), calls=%async_computation.2 | async-start | bytes 524288 | tf_op jit(solution)/shard_map/all_to_all | solution.py:100
  37.0 0.8 copy.55
  37.8 0.8 copy.53
  38.5 0.8 copy.54
  39.8 0.7 fusion.19
  40.5 6.5 %all-to-all-done.2 = bf16[16,64,128]{2,1,0:T(8,128)(2,1)S(1)} async-done(((bf16[16,64,128]{2,1,0:T(8,128)(2,1)}), bf16[16,64,128]{2,1,0:T(8,128)(2,1)S(1)}, u32[]{:S(2)}, u32[]{:S(2)}) %all-to-all-start.2) | async-done | bytes 262176 | tf_op jit(solution)/shard_map/all_to_all | solution.py:100
  47.0 3.5 %all-to-all-start.4 = ((bf16[16,64,128]{2,1,0:T(8,128)(2,1)}), bf16[16,64,128]{2,1,0:T(8,128)(2,1)S(1)}, u32[]{:S(2)}, u32[]{:S(2)}) async-start(bf16[16,64,128]{2,1,0:T(8,128)(2,1)} %bitcast.13), calls=%async_computation.4 | async-start | bytes 524288 | tf_op jit(solution)/shard_map/all_to_all | solution.py:102
  51.8 1.8 fusion.25
  53.6 6.9 %all-to-all-done.4 = bf16[16,64,128]{2,1,0:T(8,128)(2,1)S(1)} async-done(((bf16[16,64,128]{2,1,0:T(8,128)(2,1)}), bf16[16,64,128]{2,1,0:T(8,128)(2,1)S(1)}, u32[]{:S(2)}, u32[]{:S(2)}) %all-to-all-start.4) | async-done | bytes 262176 | tf_op jit(solution)/shard_map/all_to_all | solution.py:102
  60.5 3.5 %all-to-all-start.3 = ((bf16[16,64,128]{2,1,0:T(8,128)(2,1)}), bf16[16,64,128]{2,1,0:T(8,128)(2,1)S(1)}, u32[]{:S(2)}, u32[]{:S(2)}) async-start(bf16[16,64,128]{2,1,0:T(8,128)(2,1)} %bitcast.10), calls=%async_computation.3 | async-start | bytes 524288 | tf_op jit(solution)/shard_map/all_to_all | solution.py:101
  64.0 0.7 fusion.20
  65.3 8.7 %all-to-all-done.3 = bf16[16,64,128]{2,1,0:T(8,128)(2,1)S(1)} async-done(((bf16[16,64,128]{2,1,0:T(8,128)(2,1)}), bf16[16,64,128]{2,1,0:T(8,128)(2,1)S(1)}, u32[]{:S(2)}, u32[]{:S(2)}) %all-to-all-start.3) | async-done | bytes 262176 | tf_op jit(solution)/shard_map/all_to_all | solution.py:101
  74.0 3.7 %all-to-all-start.5 = ((bf16[16,64,128]{2,1,0:T(8,128)(2,1)}), bf16[16,64,128]{2,1,0:T(8,128)(2,1)S(1)}, u32[]{:S(2)}, u32[]{:S(2)}) async-start(bf16[16,64,128]{2,1,0:T(8,128)(2,1)} %bitcast.16), calls=%async_computation.5 | async-start | bytes 524288 | tf_op jit(solution)/shard_map/all_to_all | solution.py:99
  78.2 1.1 copy-done.8
  79.3 2.1 %multiply_reduce_fusion.2 = (f32[512]{0:T(512)S(1)}, f32[512,1024]{1,0:T(8,128)}) fusion(f32[512]{0:T(512)S(1)} %fusion.1, f32[512,1024]{1,0:T(8,128)S(1)} %get-tuple-element.85, f32[512]{0:T(512)S(1)} %get-tuple-element.84, f32[512,1024]{1,0:T(8,128)S(1)} %copy-done.8, bf16[512,128]{1,0:T(8,128)(2,1)S(1)} %bitcast.176, bf16[1024,128]{1,0:T(8,128)(2,1)S(1)} %bitcast.144), kind=kOutput, calls=%fused_computation.5 | convolution fusion | flops 137362944 | bytes 6690816 | tf_op jit(solution)/shard_map/dot_general | solution.py:10
  81.4 6.1 %all-to-all-done.5 = bf16[16,64,128]{2,1,0:T(8,128)(2,1)S(1)} async-done(((bf16[16,64,128]{2,1,0:T(8,128)(2,1)}), bf16[16,64,128]{2,1,0:T(8,128)(2,1)S(1)}, u32[]{:S(2)}, u32[]{:S(2)}) %all-to-all-start.5) | async-done | bytes 262176 | tf_op jit(solution)/shard_map/all_to_all | solution.py:99
  87.5 2.7 %multiply_reduce_fusion.1 = (f32[512]{0:T(512)S(1)}, f32[512]{0:T(512)S(1)}, f32[512,1024]{1,0:T(8,128)S(1)}) fusion(f32[512]{0:T(512)S(1)} %fusion.1, f32[512,1024]{1,0:T(8,128)S(1)} %get-tuple-element.85, f32[512]{0:T(512)S(1)} %get-tuple-element.84, f32[512,1024]{1,0:T(8,128)} %get-tuple-element.87, f32[512]{0:T(512)S(1)} %get-tuple-element.86, ...), kind=kOutput, calls=%fused_computation.3 | convolution fusion | flops 138411008 | bytes 6694912 | tf_op jit(solution)/shard_map/dot_general | solution.py:10
  90.3 1.2 multiply_convert_fusion
  91.6 1.1 fusion.26
  92.7 1.3 fusion.28
  97.3 1.3 multiply_convert_fusion.1
  98.7 1.0 fusion.27
  99.7 1.2 fusion.9
  101.8 2.2 %reduce.12 = bf16[1024,128]{1,0:T(8,128)(2,1)S(1)} reduce(bf16[1024,1,128]{2,1,0:T(2,128)(2,1)S(1)} %bitcast.149, bf16[]{:T(256)} %broadcast.116), dimensions={1}, to_apply=%bitcast.132.reduce_sub_computation | reduce | bytes 524290
  104.1 0.8 reshape.297
  104.8 3.8 %all-to-all-start.8 = ((bf16[16,2,4096]{2,1,0:T(2,128)(2,1)}), bf16[16,2,4096]{2,1,0:T(2,128)(2,1)S(1)}, u32[]{:S(2)}, u32[]{:S(2)}) async-start(bf16[16,2,4096]{2,1,0:T(2,128)(2,1)} %reshape.297), calls=%async_computation.8 | async-start | bytes 524288 | tf_op jit(solution)/shard_map/all_to_all | solution.py:115
  108.6 1.2 fusion.8
  109.9 1.2 multiply_reduce_fusion.6
  111.5 2.9 %reduce.13 = bf16[1024,128]{1,0:T(8,128)(2,1)} reduce(bf16[1024,1,128]{2,1,0:T(2,128)(2,1)S(1)} %bitcast.152, bf16[]{:T(256)} %broadcast.116), dimensions={1}, to_apply=%bitcast.133.reduce_sub_computation | reduce | bytes 524290
  114.4 1.7 reshape.295
  116.9 1.4 all-to-all-done.8
  118.4 4.3 %all-to-all-start.7 = ((bf16[16,2,4096]{2,1,0:T(2,128)(2,1)}), bf16[16,2,4096]{2,1,0:T(2,128)(2,1)S(1)}, u32[]{:S(2)}, u32[]{:S(2)}) async-start(bf16[16,2,4096]{2,1,0:T(2,128)(2,1)} %reshape.295), calls=%async_computation.7 | async-start | bytes 524288 | tf_op jit(solution)/shard_map/all_to_all | solution.py:114
  123.6 2.2 %reduce.11 = bf16[1024,128]{1,0:T(8,128)(2,1)S(1)} reduce(bf16[1024,1,128]{2,1,0:T(2,128)(2,1)S(1)} %bitcast.151, bf16[]{:T(256)} %broadcast.116), dimensions={1}, to_apply=%bitcast.134.reduce_sub_computation | reduce | bytes 524290
  125.8 0.8 reshape.293
  126.5 6.2 %all-to-all-done.7 = bf16[16,2,4096]{2,1,0:T(2,128)(2,1)S(1)} async-done(((bf16[16,2,4096]{2,1,0:T(2,128)(2,1)}), bf16[16,2,4096]{2,1,0:T(2,128)(2,1)S(1)}, u32[]{:S(2)}, u32[]{:S(2)}) %all-to-all-start.7) | async-done | bytes 262176 | tf_op jit(solution)/shard_map/all_to_all | solution.py:114
  132.7 3.5 %all-to-all-start.6 = ((bf16[16,2,4096]{2,1,0:T(2,128)(2,1)}), bf16[16,2,4096]{2,1,0:T(2,128)(2,1)S(1)}, u32[]{:S(2)}, u32[]{:S(2)}) async-start(bf16[16,2,4096]{2,1,0:T(2,128)(2,1)} %reshape.293), calls=%async_computation.6 | async-start | bytes 524288 | tf_op jit(solution)/shard_map/all_to_all | solution.py:113
  136.3 0.7 multiply_reduce_fusion.7
  138.5 40.5 %psum.7 = f32[2,16]{1,0:T(2,128)} all-reduce(f32[2,16]{1,0:T(2,128)S(1)} %and_select_fusion), channel_id=1, replica_groups=mesh['seq'=16,'dp'=2] {'seq','dp'}, use_global_device_ids=true, to_apply=%region_12.13 | all-reduce | flops 32 | bytes 256 | tf_op jit(solution)/shard_map/psum | solution.py:134
  180.0 0.8 copy.80
  180.8 0.9 copy_bitcast_fusion
  (103 shorter events, 10.6 us)
Async XLA Ops:
  0.6 9.3 %copy-start.21 = (bf16[2,64,1024]{2,1,0:T(8,128)(2,1)S(1)}, bf16[2,64,1024]{2,1,0:T(8,128)(2,1)}, u32[]{:S(2)}) copy-start(bf16[2,64,1024]{2,1,0:T(8,128)(2,1)} %param.19) | copy-start | bytes 786436
  0.6 10.1 %copy-start.22 = (bf16[2,64,1024]{2,1,0:T(8,128)(2,1)S(1)}, bf16[2,64,1024]{2,1,0:T(8,128)(2,1)}, u32[]{:S(2)}) copy-start(bf16[2,64,1024]{2,1,0:T(8,128)(2,1)} %param.20) | copy-start | bytes 786436
  0.7 10.2 %copy-start.23 = (bf16[2,64,1024]{2,1,0:T(8,128)(2,1)S(1)}, bf16[2,64,1024]{2,1,0:T(8,128)(2,1)}, u32[]{:S(2)}) copy-start(bf16[2,64,1024]{2,1,0:T(8,128)(2,1)} %param.21) | copy-start | bytes 786436
  2.5 17.4 %all-to-all-start = ((bf16[16,64,128]{2,1,0:T(8,128)(2,1)}), bf16[16,64,128]{2,1,0:T(8,128)(2,1)S(1)}, u32[]{:S(2)}, u32[]{:S(2)}) async-start(bf16[16,64,128]{2,1,0:T(8,128)(2,1)} %bitcast.1), calls=%async_computation | async-start | bytes 524288 | tf_op jit(solution)/shard_map/all_to_all | solution.py:97
  10.0 14.3 %copy-start.24 = (bf16[2,64,1024]{2,1,0:T(8,128)(2,1)S(1)}, bf16[2,64,1024]{2,1,0:T(8,128)(2,1)}, u32[]{:S(2)}) copy-start(bf16[2,64,1024]{2,1,0:T(8,128)(2,1)} %param.22) | copy-start | bytes 786436
  10.0 14.3 %copy-start.25 = (bf16[2,64,1024]{2,1,0:T(8,128)(2,1)S(1)}, bf16[2,64,1024]{2,1,0:T(8,128)(2,1)}, u32[]{:S(2)}) copy-start(bf16[2,64,1024]{2,1,0:T(8,128)(2,1)} %param.23) | copy-start | bytes 786436
  19.9 13.5 %all-to-all-start.1 = ((bf16[16,64,128]{2,1,0:T(8,128)(2,1)}), bf16[16,64,128]{2,1,0:T(8,128)(2,1)S(1)}, u32[]{:S(2)}, u32[]{:S(2)}) async-start(bf16[16,64,128]{2,1,0:T(8,128)(2,1)} %bitcast.4), calls=%async_computation.1 | async-start | bytes 524288 | tf_op jit(solution)/shard_map/all_to_all | solution.py:98
  33.4 13.5 %all-to-all-start.2 = ((bf16[16,64,128]{2,1,0:T(8,128)(2,1)}), bf16[16,64,128]{2,1,0:T(8,128)(2,1)S(1)}, u32[]{:S(2)}, u32[]{:S(2)}) async-start(bf16[16,64,128]{2,1,0:T(8,128)(2,1)} %bitcast.7), calls=%async_computation.2 | async-start | bytes 524288 | tf_op jit(solution)/shard_map/all_to_all | solution.py:100
  47.0 13.5 %copy-start.6 = (bf16[16,64,128]{2,1,0:T(8,128)(2,1)}, bf16[16,64,128]{2,1,0:T(8,128)(2,1)S(1)}, u32[]{:S(2)}) copy-start(bf16[16,64,128]{2,1,0:T(8,128)(2,1)S(1)} %all-to-all-done.2) | copy-start | bytes 786436
  47.0 13.5 %all-to-all-start.4 = ((bf16[16,64,128]{2,1,0:T(8,128)(2,1)}), bf16[16,64,128]{2,1,0:T(8,128)(2,1)S(1)}, u32[]{:S(2)}, u32[]{:S(2)}) async-start(bf16[16,64,128]{2,1,0:T(8,128)(2,1)} %bitcast.13), calls=%async_computation.4 | async-start | bytes 524288 | tf_op jit(solution)/shard_map/all_to_all | solution.py:102
  51.2 0.6 copy-start.13
  60.5 13.5 %all-to-all-start.3 = ((bf16[16,64,128]{2,1,0:T(8,128)(2,1)}), bf16[16,64,128]{2,1,0:T(8,128)(2,1)S(1)}, u32[]{:S(2)}, u32[]{:S(2)}) async-start(bf16[16,64,128]{2,1,0:T(8,128)(2,1)} %bitcast.10), calls=%async_computation.3 | async-start | bytes 524288 | tf_op jit(solution)/shard_map/all_to_all | solution.py:101
  64.7 22.8 %copy-start.26 = (bf16[8,64,128]{2,1,0:T(8,128)(2,1)}, bf16[8,64,128]{2,1,0:T(8,128)(2,1)S(1)}, u32[]{:S(2)}) copy-start(bf16[8,64,128]{2,1,0:T(8,128)(2,1)S(1)} %get-tuple-element.83) | copy-start | bytes 393220
  74.0 7.4 %copy-start.3 = (bf16[16,64,128]{2,1,0:T(8,128)(2,1)}, bf16[16,64,128]{2,1,0:T(8,128)(2,1)S(1)}, u32[]{:S(2)}) copy-start(bf16[16,64,128]{2,1,0:T(8,128)(2,1)S(1)} %all-to-all-done.3) | copy-start | bytes 786436
  74.0 13.5 %all-to-all-start.5 = ((bf16[16,64,128]{2,1,0:T(8,128)(2,1)}), bf16[16,64,128]{2,1,0:T(8,128)(2,1)S(1)}, u32[]{:S(2)}, u32[]{:S(2)}) async-start(bf16[16,64,128]{2,1,0:T(8,128)(2,1)} %bitcast.16), calls=%async_computation.5 | async-start | bytes 524288 | tf_op jit(solution)/shard_map/all_to_all | solution.py:99
  77.7 1.6 copy-start.8
  87.5 2.7 %copy-start.16 = (bf16[16,64,128]{2,1,0:T(8,128)(2,1)}, bf16[16,64,128]{2,1,0:T(8,128)(2,1)S(1)}, u32[]{:S(2)}) copy-start(bf16[16,64,128]{2,1,0:T(8,128)(2,1)S(1)} %all-to-all-done.5) | copy-start | bytes 786436
  87.5 2.7 %copy-start.10 = (f32[512,1024]{1,0:T(8,128)S(1)}, f32[512,1024]{1,0:T(8,128)}, u32[]{:S(2)}) copy-start(f32[512,1024]{1,0:T(8,128)} %get-tuple-element.87) | copy-start | bytes 6291460
  91.5 2.5 %copy-start.11 = (bf16[8,64,128]{2,1,0:T(8,128)(2,1)S(1)}, bf16[8,64,128]{2,1,0:T(8,128)(2,1)}, u32[]{:S(2)}) copy-start(bf16[8,64,128]{2,1,0:T(8,128)(2,1)} %get-tuple-element.78) | copy-start | bytes 393220
  91.5 2.8 %copy-start.20 = (bf16[8,64,128]{2,1,0:T(8,128)(2,1)S(1)}, bf16[8,64,128]{2,1,0:T(8,128)(2,1)}, u32[]{:S(2)}) copy-start(bf16[8,64,128]{2,1,0:T(8,128)(2,1)} %get-tuple-element.80) | copy-start | bytes 393220
  94.0 0.9 copy-start.4
  94.9 0.7 copy-start.18
  94.9 1.0 copy-start.28
  95.9 0.9 copy-start.17
  97.3 2.4 %copy-start.27 = (bf16[8,64,128]{2,1,0:T(8,128)(2,1)S(1)}, bf16[8,64,128]{2,1,0:T(8,128)(2,1)}, u32[]{:S(2)}) copy-start(bf16[8,64,128]{2,1,0:T(8,128)(2,1)} %copy-done.26) | copy-start | bytes 393220
  98.7 2.2 %copy-start = (bf16[512,512]{0,1:T(8,128)(2,1)}, bf16[512,512]{0,1:T(8,128)(2,1)S(1)}, u32[]{:S(2)}) copy-start(bf16[512,512]{0,1:T(8,128)(2,1)S(1)} %get-tuple-element.75) | copy-start | bytes 1572868
  100.9 7.7 %copy-start.2 = (bf16[512,512]{0,1:T(8,128)(2,1)S(1)}, bf16[512,512]{0,1:T(8,128)(2,1)}, u32[]{:S(2)}) copy-start(bf16[512,512]{0,1:T(8,128)(2,1)} %get-tuple-element.74) | copy-start | bytes 1572868
  100.9 7.7 %copy-start.12 = (bf16[8,64,128]{2,1,0:T(8,128)(2,1)S(1)}, bf16[8,64,128]{2,1,0:T(8,128)(2,1)}, u32[]{:S(2)}) copy-start(bf16[8,64,128]{2,1,0:T(8,128)(2,1)} %get-tuple-element.78) | copy-start | bytes 393220
  100.9 9.0 %copy-start.5 = (bf16[16,64,128]{2,1,0:T(8,128)(2,1)S(1)}, bf16[16,64,128]{2,1,0:T(8,128)(2,1)}, u32[]{:S(2)}) copy-start(bf16[16,64,128]{2,1,0:T(8,128)(2,1)} %copy-done.3) | copy-start | bytes 786436
  100.9 9.0 %copy-start.9 = (f32[1024,128]{1,0:T(8,128)S(1)}, f32[1024,128]{1,0:T(8,128)}, u32[]{:S(2)}) copy-start(f32[1024,128]{1,0:T(8,128)} %fusion.28) | copy-start | bytes 1572868
  100.9 9.0 %copy-start.14 = (bf16[8,64,128]{2,1,0:T(8,128)(2,1)S(1)}, bf16[8,64,128]{2,1,0:T(8,128)(2,1)}, u32[]{:S(2)}) copy-start(bf16[8,64,128]{2,1,0:T(8,128)(2,1)} %copy-done.13) | copy-start | bytes 393220
  104.8 13.5 %all-to-all-start.8 = ((bf16[16,2,4096]{2,1,0:T(2,128)(2,1)}), bf16[16,2,4096]{2,1,0:T(2,128)(2,1)S(1)}, u32[]{:S(2)}, u32[]{:S(2)}) async-start(bf16[16,2,4096]{2,1,0:T(2,128)(2,1)} %reshape.297), calls=%async_computation.8 | async-start | bytes 524288 | tf_op jit(solution)/shard_map/all_to_all | solution.py:115
  109.9 6.2 %copy-start.1 = (bf16[512,512]{0,1:T(8,128)(2,1)S(1)}, bf16[512,512]{0,1:T(8,128)(2,1)}, u32[]{:S(2)}) copy-start(bf16[512,512]{0,1:T(8,128)(2,1)} %copy-done) | copy-start | bytes 1572868
  111.1 5.4 %copy-start.15 = (f32[512,128]{1,0:T(8,128)S(1)}, f32[512,128]{1,0:T(8,128)}, u32[]{:S(2)}) copy-start(f32[512,128]{1,0:T(8,128)} %fusion.26) | copy-start | bytes 786436
  116.5 6.2 %copy-start.19 = (bf16[8,64,128]{2,1,0:T(8,128)(2,1)S(1)}, bf16[8,64,128]{2,1,0:T(8,128)(2,1)}, u32[]{:S(2)}) copy-start(bf16[8,64,128]{2,1,0:T(8,128)(2,1)} %copy-done.18) | copy-start | bytes 393220
  118.4 14.3 %all-to-all-start.7 = ((bf16[16,2,4096]{2,1,0:T(2,128)(2,1)}), bf16[16,2,4096]{2,1,0:T(2,128)(2,1)S(1)}, u32[]{:S(2)}, u32[]{:S(2)}) async-start(bf16[16,2,4096]{2,1,0:T(2,128)(2,1)} %reshape.295), calls=%async_computation.7 | async-start | bytes 524288 | tf_op jit(solution)/shard_map/all_to_all | solution.py:114
  123.1 13.2 %copy-start.7 = (bf16[16,64,128]{2,1,0:T(8,128)(2,1)S(1)}, bf16[16,64,128]{2,1,0:T(8,128)(2,1)}, u32[]{:S(2)}) copy-start(bf16[16,64,128]{2,1,0:T(8,128)(2,1)} %copy-done.6) | copy-start | bytes 786436
  123.1 15.3 %copy-start.29 = (pred[16]{0:T(512)(128)(4,1)S(1)}, pred[16]{0:T(512)(128)(4,1)}, u32[]{:S(2)}) copy-start(pred[16]{0:T(512)(128)(4,1)} %iota_compare_fusion.2) | copy-start | bytes 52
  132.7 47.0 %all-to-all-start.6 = ((bf16[16,2,4096]{2,1,0:T(2,128)(2,1)}), bf16[16,2,4096]{2,1,0:T(2,128)(2,1)S(1)}, u32[]{:S(2)}, u32[]{:S(2)}) async-start(bf16[16,2,4096]{2,1,0:T(2,128)(2,1)} %reshape.293), calls=%async_computation.6 | async-start | bytes 524288 | tf_op jit(solution)/shard_map/all_to_all | solution.py:113
where the time goes:
time: 183 us; the launch traced here: 182 us
  waiting for transfers between devices  53.8 us (29%)
  blocking collectives  40.5 us (22%)
  starting transfers between devices  36.8 us (20%)
  local copies, waits for them, and re-layouts  18.6 us (10%)
  matrix products  17.2 us (9%)
  other arithmetic  12 us (7%)
  between operations  2.68 us (1%)
    psum x1, blocking collectives, local(): curvature = lax.psum(board, ('seq', 'dp'))  40.5 us
    unnamed x76, local copies, waits for them, and re-layouts  9.05 us
    all_to_all x1, waiting for transfers between devices, local(): lax.all_to_all(to_items(queries), 'seq', split_axis=0, concat_axis=1, til...  9 us
    all_to_all x1, waiting for transfers between devices, local(): lax.all_to_all(to_items(key_rows), 'seq', split_axis=0, concat_axis=1, ti...  9 us
    all_to_all x1, waiting for transfers between devices, local(): lax.all_to_all(to_items(key_tangent), 'seq', split_axis=0, concat_axis=1,...  8.73 us
    dot_general x8, matrix products, inner_rows(): lax.dot_general(left, right, (((1,), (1,)), ((), ())), preferred_element_...  8.68 us
    all_to_all x1, starting transfers between devices, local(): lax.all_to_all(to_items(queries), 'seq', split_axis=0, concat_axis=1, til...  7.39 us
    unnamed x3, other arithmetic  7.33 us
  transfers between devices with their start and end apart: 9, of which 8 were waited for; matrix products, arithmetic and copies ran while one was open for 14% of the time, Pallas kernels for 0%

commit v1 on v0

--- a/solution.py
+++ b/solution.py
@@ -131,7 +131,7 @@
     head_here = lax.axis_index("dp") * local_heads + global_item % local_heads
     hit = jnp.logical_and(batch_index == batch_here, head_index == head_here)
     board = jnp.where(hit, kappas[item], 0.0)
-    curvature = lax.psum(board, ("seq", "dp"))
+    curvature = jnp.sum(lax.all_gather(board, ("seq", "dp")), axis=0)
     return (outputs[0], outputs[1], outputs[2], curvature)
 
 

time: 183 us -> 212 us (1.16)
  blocking collectives: 40.5 us -> 68.7 us
    all_gather x0 -> x1, blocking collectives: none -> 68.7 us  [local(): curvature = jnp.sum(lax.all_gather(board, ('seq', 'dp')), axis=0)]
    psum x1 -> x0, blocking collectives: 40.5 us -> none  [local(): curvature = lax.psum(board, ('seq', 'dp'))]
  transfers between devices with their start and end apart: 9 -> 9, of which waited for: 8 -> 8; matrix products, arithmetic and copies ran while one was open for 14% -> 12% of each run, Pallas kernels for 0% -> 0%
where the time goes in v1:
time: 212 us; the launch traced here: 210 us
  blocking collectives  68.7 us (32%)
  waiting for transfers between devices  53.8 us (25%)
  starting transfers between devices  36.8 us (17%)
  local copies, waits for them, and re-layouts  18.6 us (9%)
  matrix products  17.2 us (8%)
  other arithmetic  12.6 us (6%)
  between operations  2.68 us (1%)
    all_gather x1, blocking collectives, local(): curvature = jnp.sum(lax.all_gather(board, ('seq', 'dp')), axis=0)  68.7 us
    unnamed x76, local copies, waits for them, and re-layouts  9.05 us
    all_to_all x1, waiting for transfers between devices, local(): lax.all_to_all(to_items(queries), 'seq', split_axis=0, concat_axis=1, til...  9 us
    all_to_all x1, waiting for transfers between devices, local(): lax.all_to_all(to_items(key_rows), 'seq', split_axis=0, concat_axis=1, ti...  9 us
    all_to_all x1, waiting for transfers between devices, local(): lax.all_to_all(to_items(key_tangent), 'seq', split_axis=0, concat_axis=1,...  8.73 us
    dot_general x8, matrix products, inner_rows(): lax.dot_general(left, right, (((1,), (1,)), ((), ())), preferred_element_...  8.68 us
    all_to_all x1, starting transfers between devices, local(): lax.all_to_all(to_items(queries), 'seq', split_axis=0, concat_axis=1, til...  7.39 us
    unnamed x3, other arithmetic  7.33 us
  transfers between devices with their start and end apart: 9, of which 8 were waited for; matrix products, arithmetic and copies ran while one was open for 12% of the time, Pallas kernels for 0%

profile of v1, /device:TPU:0, one launch (start us, length us, event | category | flops | bytes accessed | tf_op | source)
XLA Modules:
  0.0 210.4 jit_solution(11657384715683602550)
XLA Ops:
  0.7 1.1 copy.68
  1.8 0.8 copy.50
  2.5 7.4 %all-to-all-start = ((bf16[16,64,128]{2,1,0:T(8,128)(2,1)}), bf16[16,64,128]{2,1,0:T(8,128)(2,1)S(1)}, u32[]{:S(2)}, u32[]{:S(2)}) async-start(bf16[16,64,128]{2,1,0:T(8,128)(2,1)} %bitcast.1), calls=%async_computation | async-start | bytes 524288 | tf_op jit(solution)/shard_map/all_to_all | solution.py:97
  10.0 0.8 copy.51
  10.9 9.0 %all-to-all-done = bf16[16,64,128]{2,1,0:T(8,128)(2,1)S(1)} async-done(((bf16[16,64,128]{2,1,0:T(8,128)(2,1)}), bf16[16,64,128]{2,1,0:T(8,128)(2,1)S(1)}, u32[]{:S(2)}, u32[]{:S(2)}) %all-to-all-start) | async-done | bytes 262176 | tf_op jit(solution)/shard_map/all_to_all | solution.py:97
  19.9 3.5 %all-to-all-start.1 = ((bf16[16,64,128]{2,1,0:T(8,128)(2,1)}), bf16[16,64,128]{2,1,0:T(8,128)(2,1)S(1)}, u32[]{:S(2)}, u32[]{:S(2)}) async-start(bf16[16,64,128]{2,1,0:T(8,128)(2,1)} %bitcast.4), calls=%async_computation.1 | async-start | bytes 524288 | tf_op jit(solution)/shard_map/all_to_all | solution.py:98
  23.5 0.8 copy.52
  24.4 9.0 %all-to-all-done.1 = bf16[16,64,128]{2,1,0:T(8,128)(2,1)S(1)} async-done(((bf16[16,64,128]{2,1,0:T(8,128)(2,1)}), bf16[16,64,128]{2,1,0:T(8,128)(2,1)S(1)}, u32[]{:S(2)}, u32[]{:S(2)}) %all-to-all-start.1) | async-done | bytes 262176 | tf_op jit(solution)/shard_map/all_to_all | solution.py:98
  33.4 3.5 %all-to-all-start.2 = ((bf16[16,64,128]{2,1,0:T(8,128)(2,1)}), bf16[16,64,128]{2,1,0:T(8,128)(2,1)S(1)}, u32[]{:S(2)}, u32[]{:S(2)}) async-start(bf16[16,64,128]{2,1,0:T(8,128)(2,1)} %bitcast.7), calls=%async_computation.2 | async-start | bytes 524288 | tf_op jit(solution)/shard_map/all_to_all | solution.py:100
  37.0 0.8 copy.55
  37.8 0.8 copy.53
  38.5 0.8 copy.54
  39.8 0.7 fusion.19
  40.5 6.5 %all-to-all-done.2 = bf16[16,64,128]{2,1,0:T(8,128)(2,1)S(1)} async-done(((bf16[16,64,128]{2,1,0:T(8,128)(2,1)}), bf16[16,64,128]{2,1,0:T(8,128)(2,1)S(1)}, u32[]{:S(2)}, u32[]{:S(2)}) %all-to-all-start.2) | async-done | bytes 262176 | tf_op jit(solution)/shard_map/all_to_all | solution.py:100
  47.0 3.5 %all-to-all-start.4 = ((bf16[16,64,128]{2,1,0:T(8,128)(2,1)}), bf16[16,64,128]{2,1,0:T(8,128)(2,1)S(1)}, u32[]{:S(2)}, u32[]{:S(2)}) async-start(bf16[16,64,128]{2,1,0:T(8,128)(2,1)} %bitcast.13), calls=%async_computation.4 | async-start | bytes 524288 | tf_op jit(solution)/shard_map/all_to_all | solution.py:102
  51.8 1.8 fusion.25
  53.6 6.9 %all-to-all-done.4 = bf16[16,64,128]{2,1,0:T(8,128)(2,1)S(1)} async-done(((bf16[16,64,128]{2,1,0:T(8,128)(2,1)}), bf16[16,64,128]{2,1,0:T(8,128)(2,1)S(1)}, u32[]{:S(2)}, u32[]{:S(2)}) %all-to-all-start.4) | async-done | bytes 262176 | tf_op jit(solution)/shard_map/all_to_all | solution.py:102
  60.5 3.5 %all-to-all-start.3 = ((bf16[16,64,128]{2,1,0:T(8,128)(2,1)}), bf16[16,64,128]{2,1,0:T(8,128)(2,1)S(1)}, u32[]{:S(2)}, u32[]{:S(2)}) async-start(bf16[16,64,128]{2,1,0:T(8,128)(2,1)} %bitcast.10), calls=%async_computation.3 | async-start | bytes 524288 | tf_op jit(solution)/shard_map/all_to_all | solution.py:101
  64.0 0.7 fusion.20
  65.3 8.7 %all-to-all-done.3 = bf16[16,64,128]{2,1,0:T(8,128)(2,1)S(1)} async-done(((bf16[16,64,128]{2,1,0:T(8,128)(2,1)}), bf16[16,64,128]{2,1,0:T(8,128)(2,1)S(1)}, u32[]{:S(2)}, u32[]{:S(2)}) %all-to-all-start.3) | async-done | bytes 262176 | tf_op jit(solution)/shard_map/all_to_all | solution.py:101
  74.0 3.7 %all-to-all-start.5 = ((bf16[16,64,128]{2,1,0:T(8,128)(2,1)}), bf16[16,64,128]{2,1,0:T(8,128)(2,1)S(1)}, u32[]{:S(2)}, u32[]{:S(2)}) async-start(bf16[16,64,128]{2,1,0:T(8,128)(2,1)} %bitcast.16), calls=%async_computation.5 | async-start | bytes 524288 | tf_op jit(solution)/shard_map/all_to_all | solution.py:99
  78.2 1.1 copy-done.8
  79.3 2.1 %multiply_reduce_fusion.2 = (f32[512]{0:T(512)S(1)}, f32[512,1024]{1,0:T(8,128)}) fusion(f32[512]{0:T(512)S(1)} %fusion.1, f32[512,1024]{1,0:T(8,128)S(1)} %get-tuple-element.85, f32[512]{0:T(512)S(1)} %get-tuple-element.84, f32[512,1024]{1,0:T(8,128)S(1)} %copy-done.8, bf16[512,128]{1,0:T(8,128)(2,1)S(1)} %bitcast.176, bf16[1024,128]{1,0:T(8,128)(2,1)S(1)} %bitcast.144), kind=kOutput, calls=%fused_computation.5 | convolution fusion | flops 137362944 | bytes 6690816 | tf_op jit(solution)/shard_map/dot_general | solution.py:10
  81.4 6.1 %all-to-all-done.5 = bf16[16,64,128]{2,1,0:T(8,128)(2,1)S(1)} async-done(((bf16[16,64,128]{2,1,0:T(8,128)(2,1)}), bf16[16,64,128]{2,1,0:T(8,128)(2,1)S(1)}, u32[]{:S(2)}, u32[]{:S(2)}) %all-to-all-start.5) | async-done | bytes 262176 | tf_op jit(solution)/shard_map/all_to_all | solution.py:99
  87.5 2.7 %multiply_reduce_fusion.1 = (f32[512]{0:T(512)S(1)}, f32[512]{0:T(512)S(1)}, f32[512,1024]{1,0:T(8,128)S(1)}) fusion(f32[512]{0:T(512)S(1)} %fusion.1, f32[512,1024]{1,0:T(8,128)S(1)} %get-tuple-element.85, f32[512]{0:T(512)S(1)} %get-tuple-element.84, f32[512,1024]{1,0:T(8,128)} %get-tuple-element.87, f32[512]{0:T(512)S(1)} %get-tuple-element.86, ...), kind=kOutput, calls=%fused_computation.3 | convolution fusion | flops 138411008 | bytes 6694912 | tf_op jit(solution)/shard_map/dot_general | solution.py:10
  90.3 1.2 multiply_convert_fusion
  91.6 1.1 fusion.26
  92.7 1.3 fusion.28
  97.3 1.3 multiply_convert_fusion.1
  98.7 1.0 fusion.27
  99.7 1.2 fusion.9
  101.8 2.2 %reduce.12 = bf16[1024,128]{1,0:T(8,128)(2,1)S(1)} reduce(bf16[1024,1,128]{2,1,0:T(2,128)(2,1)S(1)} %bitcast.149, bf16[]{:T(256)} %broadcast.167), dimensions={1}, to_apply=%bitcast.132.reduce_sub_computation | reduce | bytes 524290
  104.1 0.8 reshape.343
  104.8 3.8 %all-to-all-start.8 = ((bf16[16,2,4096]{2,1,0:T(2,128)(2,1)}), bf16[16,2,4096]{2,1,0:T(2,128)(2,1)S(1)}, u32[]{:S(2)}, u32[]{:S(2)}) async-start(bf16[16,2,4096]{2,1,0:T(2,128)(2,1)} %reshape.343), calls=%async_computation.8 | async-start | bytes 524288 | tf_op jit(solution)/shard_map/all_to_all | solution.py:115
  108.6 1.2 fusion.8
  109.9 1.2 multiply_reduce_fusion.6
  111.5 2.9 %reduce.13 = bf16[1024,128]{1,0:T(8,128)(2,1)} reduce(bf16[1024,1,128]{2,1,0:T(2,128)(2,1)S(1)} %bitcast.152, bf16[]{:T(256)} %broadcast.167), dimensions={1}, to_apply=%bitcast.133.reduce_sub_computation | reduce | bytes 524290
  114.4 1.7 reshape.341
  116.9 1.4 all-to-all-done.8
  118.4 4.3 %all-to-all-start.7 = ((bf16[16,2,4096]{2,1,0:T(2,128)(2,1)}), bf16[16,2,4096]{2,1,0:T(2,128)(2,1)S(1)}, u32[]{:S(2)}, u32[]{:S(2)}) async-start(bf16[16,2,4096]{2,1,0:T(2,128)(2,1)} %reshape.341), calls=%async_computation.7 | async-start | bytes 524288 | tf_op jit(solution)/shard_map/all_to_all | solution.py:114
  123.6 2.2 %reduce.11 = bf16[1024,128]{1,0:T(8,128)(2,1)S(1)} reduce(bf16[1024,1,128]{2,1,0:T(2,128)(2,1)S(1)} %bitcast.151, bf16[]{:T(256)} %broadcast.167), dimensions={1}, to_apply=%bitcast.134.reduce_sub_computation | reduce | bytes 524290
  125.8 0.8 reshape.339
  126.5 6.2 %all-to-all-done.7 = bf16[16,2,4096]{2,1,0:T(2,128)(2,1)S(1)} async-done(((bf16[16,2,4096]{2,1,0:T(2,128)(2,1)}), bf16[16,2,4096]{2,1,0:T(2,128)(2,1)S(1)}, u32[]{:S(2)}, u32[]{:S(2)}) %all-to-all-start.7) | async-done | bytes 262176 | tf_op jit(solution)/shard_map/all_to_all | solution.py:114
  132.7 3.5 %all-to-all-start.6 = ((bf16[16,2,4096]{2,1,0:T(2,128)(2,1)}), bf16[16,2,4096]{2,1,0:T(2,128)(2,1)S(1)}, u32[]{:S(2)}, u32[]{:S(2)}) async-start(bf16[16,2,4096]{2,1,0:T(2,128)(2,1)} %reshape.339), calls=%async_computation.6 | async-start | bytes 524288 | tf_op jit(solution)/shard_map/all_to_all | solution.py:113
  136.3 0.7 multiply_reduce_fusion.7
  138.5 68.7 %all_gather.4 = f32[32,2,16]{2,1,0:T(2,128)S(1)} all-gather(f32[1,2,16]{2,1,0:T(2,128)S(1)} %and_select_fusion), channel_id=1, replica_groups=mesh['seq'=16,'dp'=2] {'seq','dp'}, dimensions={0}, use_global_device_ids=true | all-gather | bytes 4224 | tf_op jit(solution)/shard_map/all_gather | solution.py:134
  208.8 0.8 copy.80
  209.5 0.9 copy_bitcast_fusion
  (104 shorter events, 11.2 us)
Async XLA Ops:
  0.6 9.3 %copy-start.21 = (bf16[2,64,1024]{2,1,0:T(8,128)(2,1)S(1)}, bf16[2,64,1024]{2,1,0:T(8,128)(2,1)}, u32[]{:S(2)}) copy-start(bf16[2,64,1024]{2,1,0:T(8,128)(2,1)} %param.19) | copy-start | bytes 786436
  0.6 10.1 %copy-start.22 = (bf16[2,64,1024]{2,1,0:T(8,128)(2,1)S(1)}, bf16[2,64,1024]{2,1,0:T(8,128)(2,1)}, u32[]{:S(2)}) copy-start(bf16[2,64,1024]{2,1,0:T(8,128)(2,1)} %param.20) | copy-start | bytes 786436
  0.7 10.2 %copy-start.23 = (bf16[2,64,1024]{2,1,0:T(8,128)(2,1)S(1)}, bf16[2,64,1024]{2,1,0:T(8,128)(2,1)}, u32[]{:S(2)}) copy-start(bf16[2,64,1024]{2,1,0:T(8,128)(2,1)} %param.21) | copy-start | bytes 786436
  2.5 17.4 %all-to-all-start = ((bf16[16,64,128]{2,1,0:T(8,128)(2,1)}), bf16[16,64,128]{2,1,0:T(8,128)(2,1)S(1)}, u32[]{:S(2)}, u32[]{:S(2)}) async-start(bf16[16,64,128]{2,1,0:T(8,128)(2,1)} %bitcast.1), calls=%async_computation | async-start | bytes 524288 | tf_op jit(solution)/shard_map/all_to_all | solution.py:97
  10.0 14.3 %copy-start.24 = (bf16[2,64,1024]{2,1,0:T(8,128)(2,1)S(1)}, bf16[2,64,1024]{2,1,0:T(8,128)(2,1)}, u32[]{:S(2)}) copy-start(bf16[2,64,1024]{2,1,0:T(8,128)(2,1)} %param.22) | copy-start | bytes 786436
  10.0 14.3 %copy-start.25 = (bf16[2,64,1024]{2,1,0:T(8,128)(2,1)S(1)}, bf16[2,64,1024]{2,1,0:T(8,128)(2,1)}, u32[]{:S(2)}) copy-start(bf16[2,64,1024]{2,1,0:T(8,128)(2,1)} %param.23) | copy-start | bytes 786436
  19.9 13.5 %all-to-all-start.1 = ((bf16[16,64,128]{2,1,0:T(8,128)(2,1)}), bf16[16,64,128]{2,1,0:T(8,128)(2,1)S(1)}, u32[]{:S(2)}, u32[]{:S(2)}) async-start(bf16[16,64,128]{2,1,0:T(8,128)(2,1)} %bitcast.4), calls=%async_computation.1 | async-start | bytes 524288 | tf_op jit(solution)/shard_map/all_to_all | solution.py:98
  33.4 13.5 %all-to-all-start.2 = ((bf16[16,64,128]{2,1,0:T(8,128)(2,1)}), bf16[16,64,128]{2,1,0:T(8,128)(2,1)S(1)}, u32[]{:S(2)}, u32[]{:S(2)}) async-start(bf16[16,64,128]{2,1,0:T(8,128)(2,1)} %bitcast.7), calls=%async_computation.2 | async-start | bytes 524288 | tf_op jit(solution)/shard_map/all_to_all | solution.py:100
  47.0 13.5 %copy-start.6 = (bf16[16,64,128]{2,1,0:T(8,128)(2,1)}, bf16[16,64,128]{2,1,0:T(8,128)(2,1)S(1)}, u32[]{:S(2)}) copy-start(bf16[16,64,128]{2,1,0:T(8,128)(2,1)S(1)} %all-to-all-done.2) | copy-start | bytes 786436
  47.0 13.5 %all-to-all-start.4 = ((bf16[16,64,128]{2,1,0:T(8,128)(2,1)}), bf16[16,64,128]{2,1,0:T(8,128)(2,1)S(1)}, u32[]{:S(2)}, u32[]{:S(2)}) async-start(bf16[16,64,128]{2,1,0:T(8,128)(2,1)} %bitcast.13), calls=%async_computation.4 | async-start | bytes 524288 | tf_op jit(solution)/shard_map/all_to_all | solution.py:102
  51.2 0.6 copy-start.13
  60.5 13.5 %all-to-all-start.3 = ((bf16[16,64,128]{2,1,0:T(8,128)(2,1)}), bf16[16,64,128]{2,1,0:T(8,128)(2,1)S(1)}, u32[]{:S(2)}, u32[]{:S(2)}) async-start(bf16[16,64,128]{2,1,0:T(8,128)(2,1)} %bitcast.10), calls=%async_computation.3 | async-start | bytes 524288 | tf_op jit(solution)/shard_map/all_to_all | solution.py:101
  64.7 22.8 %copy-start.26 = (bf16[8,64,128]{2,1,0:T(8,128)(2,1)}, bf16[8,64,128]{2,1,0:T(8,128)(2,1)S(1)}, u32[]{:S(2)}) copy-start(bf16[8,64,128]{2,1,0:T(8,128)(2,1)S(1)} %get-tuple-element.83) | copy-start | bytes 393220
  74.0 7.4 %copy-start.3 = (bf16[16,64,128]{2,1,0:T(8,128)(2,1)}, bf16[16,64,128]{2,1,0:T(8,128)(2,1)S(1)}, u32[]{:S(2)}) copy-start(bf16[16,64,128]{2,1,0:T(8,128)(2,1)S(1)} %all-to-all-done.3) | copy-start | bytes 786436
  74.0 13.5 %all-to-all-start.5 = ((bf16[16,64,128]{2,1,0:T(8,128)(2,1)}), bf16[16,64,128]{2,1,0:T(8,128)(2,1)S(1)}, u32[]{:S(2)}, u32[]{:S(2)}) async-start(bf16[16,64,128]{2,1,0:T(8,128)(2,1)} %bitcast.16), calls=%async_computation.5 | async-start | bytes 524288 | tf_op jit(solution)/shard_map/all_to_all | solution.py:99
  77.7 1.6 copy-start.8
  87.5 2.7 %copy-start.16 = (bf16[16,64,128]{2,1,0:T(8,128)(2,1)}, bf16[16,64,128]{2,1,0:T(8,128)(2,1)S(1)}, u32[]{:S(2)}) copy-start(bf16[16,64,128]{2,1,0:T(8,128)(2,1)S(1)} %all-to-all-done.5) | copy-start | bytes 786436
  87.5 2.7 %copy-start.10 = (f32[512,1024]{1,0:T(8,128)S(1)}, f32[512,1024]{1,0:T(8,128)}, u32[]{:S(2)}) copy-start(f32[512,1024]{1,0:T(8,128)} %get-tuple-element.87) | copy-start | bytes 6291460
  91.5 2.5 %copy-start.11 = (bf16[8,64,128]{2,1,0:T(8,128)(2,1)S(1)}, bf16[8,64,128]{2,1,0:T(8,128)(2,1)}, u32[]{:S(2)}) copy-start(bf16[8,64,128]{2,1,0:T(8,128)(2,1)} %get-tuple-element.78) | copy-start | bytes 393220
  91.5 2.8 %copy-start.20 = (bf16[8,64,128]{2,1,0:T(8,128)(2,1)S(1)}, bf16[8,64,128]{2,1,0:T(8,128)(2,1)}, u32[]{:S(2)}) copy-start(bf16[8,64,128]{2,1,0:T(8,128)(2,1)} %get-tuple-element.80) | copy-start | bytes 393220
  94.0 0.9 copy-start.4
  94.9 0.7 copy-start.18
  94.9 1.0 copy-start.28
  95.9 0.9 copy-start.17
  97.3 2.4 %copy-start.27 = (bf16[8,64,128]{2,1,0:T(8,128)(2,1)S(1)}, bf16[8,64,128]{2,1,0:T(8,128)(2,1)}, u32[]{:S(2)}) copy-start(bf16[8,64,128]{2,1,0:T(8,128)(2,1)} %copy-done.26) | copy-start | bytes 393220
  98.7 2.2 %copy-start = (bf16[512,512]{0,1:T(8,128)(2,1)}, bf16[512,512]{0,1:T(8,128)(2,1)S(1)}, u32[]{:S(2)}) copy-start(bf16[512,512]{0,1:T(8,128)(2,1)S(1)} %get-tuple-element.75) | copy-start | bytes 1572868
  100.9 7.7 %copy-start.2 = (bf16[512,512]{0,1:T(8,128)(2,1)S(1)}, bf16[512,512]{0,1:T(8,128)(2,1)}, u32[]{:S(2)}) copy-start(bf16[512,512]{0,1:T(8,128)(2,1)} %get-tuple-element.74) | copy-start | bytes 1572868
  100.9 7.7 %copy-start.12 = (bf16[8,64,128]{2,1,0:T(8,128)(2,1)S(1)}, bf16[8,64,128]{2,1,0:T(8,128)(2,1)}, u32[]{:S(2)}) copy-start(bf16[8,64,128]{2,1,0:T(8,128)(2,1)} %get-tuple-element.78) | copy-start | bytes 393220
  100.9 9.0 %copy-start.5 = (bf16[16,64,128]{2,1,0:T(8,128)(2,1)S(1)}, bf16[16,64,128]{2,1,0:T(8,128)(2,1)}, u32[]{:S(2)}) copy-start(bf16[16,64,128]{2,1,0:T(8,128)(2,1)} %copy-done.3) | copy-start | bytes 786436
  100.9 9.0 %copy-start.9 = (f32[1024,128]{1,0:T(8,128)S(1)}, f32[1024,128]{1,0:T(8,128)}, u32[]{:S(2)}) copy-start(f32[1024,128]{1,0:T(8,128)} %fusion.28) | copy-start | bytes 1572868
  100.9 9.0 %copy-start.14 = (bf16[8,64,128]{2,1,0:T(8,128)(2,1)S(1)}, bf16[8,64,128]{2,1,0:T(8,128)(2,1)}, u32[]{:S(2)}) copy-start(bf16[8,64,128]{2,1,0:T(8,128)(2,1)} %copy-done.13) | copy-start | bytes 393220
  104.8 13.5 %all-to-all-start.8 = ((bf16[16,2,4096]{2,1,0:T(2,128)(2,1)}), bf16[16,2,4096]{2,1,0:T(2,128)(2,1)S(1)}, u32[]{:S(2)}, u32[]{:S(2)}) async-start(bf16[16,2,4096]{2,1,0:T(2,128)(2,1)} %reshape.343), calls=%async_computation.8 | async-start | bytes 524288 | tf_op jit(solution)/shard_map/all_to_all | solution.py:115
  109.9 6.2 %copy-start.1 = (bf16[512,512]{0,1:T(8,128)(2,1)S(1)}, bf16[512,512]{0,1:T(8,128)(2,1)}, u32[]{:S(2)}) copy-start(bf16[512,512]{0,1:T(8,128)(2,1)} %copy-done) | copy-start | bytes 1572868
  111.1 5.4 %copy-start.15 = (f32[512,128]{1,0:T(8,128)S(1)}, f32[512,128]{1,0:T(8,128)}, u32[]{:S(2)}) copy-start(f32[512,128]{1,0:T(8,128)} %fusion.26) | copy-start | bytes 786436
  116.5 6.2 %copy-start.19 = (bf16[8,64,128]{2,1,0:T(8,128)(2,1)S(1)}, bf16[8,64,128]{2,1,0:T(8,128)(2,1)}, u32[]{:S(2)}) copy-start(bf16[8,64,128]{2,1,0:T(8,128)(2,1)} %copy-done.18) | copy-start | bytes 393220
  118.4 14.3 %all-to-all-start.7 = ((bf16[16,2,4096]{2,1,0:T(2,128)(2,1)}), bf16[16,2,4096]{2,1,0:T(2,128)(2,1)S(1)}, u32[]{:S(2)}, u32[]{:S(2)}) async-start(bf16[16,2,4096]{2,1,0:T(2,128)(2,1)} %reshape.341), calls=%async_computation.7 | async-start | bytes 524288 | tf_op jit(solution)/shard_map/all_to_all | solution.py:114
  123.1 13.2 %copy-start.7 = (bf16[16,64,128]{2,1,0:T(8,128)(2,1)S(1)}, bf16[16,64,128]{2,1,0:T(8,128)(2,1)}, u32[]{:S(2)}) copy-start(bf16[16,64,128]{2,1,0:T(8,128)(2,1)} %copy-done.6) | copy-start | bytes 786436
  123.1 15.3 %copy-start.29 = (pred[16]{0:T(512)(128)(4,1)S(1)}, pred[16]{0:T(512)(128)(4,1)}, u32[]{:S(2)}) copy-start(pred[16]{0:T(512)(128)(4,1)} %iota_compare_fusion.2) | copy-start | bytes 52
  132.7 75.7 %all-to-all-start.6 = ((bf16[16,2,4096]{2,1,0:T(2,128)(2,1)}), bf16[16,2,4096]{2,1,0:T(2,128)(2,1)S(1)}, u32[]{:S(2)}, u32[]{:S(2)}) async-start(bf16[16,2,4096]{2,1,0:T(2,128)(2,1)} %reshape.339), calls=%async_computation.6 | async-start | bytes 524288 | tf_op jit(solution)/shard_map/all_to_all | solution.py:113
